TPU v7x, 32 devices: a whole 2x2x4 slice. The times are simulated.
32 devices in a mesh: dp: 8 (over z, x), tensor: 4 (over y, core).
Axes of the slice: x: 2, y: 2, z: 4, core: 2. Of those that a mesh axis runs over, the one named last changes fastest.
Arguments:
- tokens: bfloat16 [16384, 768], P(('dp', 'tensor')), may hold values from -6 to 6
- w_query: bfloat16 [768, 768], P(None, 'tensor'), may hold values from -0.3125 to 0.3125
- w_key: bfloat16 [768, 768], P(None, 'tensor'), may hold values from -0.3125 to 0.3125
- w_value: bfloat16 [768, 768], P(None, 'tensor'), may hold values from -0.21875 to 0.21875
- b_query: bfloat16 [768], P('tensor'), may hold values from -3 to 3
- b_value: bfloat16 [768], P('tensor'), may hold values from -3 to 3
- w_output: bfloat16 [768, 768], P('tensor'), may hold values from -0.375 to 0.375
- b_output: bfloat16 [768], replicated, may hold values from -3 to 3
- first_gain: bfloat16 [768], replicated, may hold values from 0.5 to 1.5
- first_shift: bfloat16 [768], replicated, may hold values from -3 to 3
- w_up: bfloat16 [768, 3072], P(None, 'tensor'), may hold values from -0.21875 to 0.21875
- b_up: bfloat16 [3072], P('tensor'), may hold values from -3 to 3
- w_down: bfloat16 [3072, 768], P('tensor'), may hold values from -0.15625 to 0.15625
- b_down: bfloat16 [768], replicated, may hold values from -3 to 3
- second_gain: bfloat16 [768], replicated, may hold values from 0.5 to 1.5
- second_shift: bfloat16 [768], replicated, may hold values from -3 to 3
- cotangent: bfloat16 [16384, 768], P(('dp', 'tensor')), may hold values from -24 to 24, as said below
Outputs:
- layer_out: bfloat16 [16384, 768], P(('dp', 'tensor'))
- grad_tokens: bfloat16 [16384, 768], P(('dp', 'tensor'))
- grad_w_query: float32 [768, 768], P(None, 'tensor')
- grad_w_key: float32 [768, 768], P(None, 'tensor')
- grad_w_value: float32 [768, 768], P(None, 'tensor')
- grad_b_query: float32 [768], P('tensor')
- grad_b_value: float32 [768], P('tensor')
- grad_w_output: float32 [768, 768], P('tensor')
- grad_b_output: float32 [768], replicated
- grad_first_gain: float32 [768], replicated
- grad_first_shift: float32 [768], replicated
- grad_w_up: float32 [768, 3072], P(None, 'tensor')
- grad_b_up: float32 [3072], P('tensor')
- grad_w_down: float32 [3072, 768], P('tensor')
- grad_b_down: float32 [768], replicated
- grad_second_gain: float32 [768], replicated
- grad_second_shift: float32 [768], replicated
Inputs may be any that keep to these rules, and one draw needn't show every extreme that they name: cotangent of the layer's output.
All inputs are finite; a program needn't handle non-finite values.
Results may differ from a plain program's by a relative error of at most 0.013.
The roundings to bfloat16 on the way count: a program that leaves them out, or rounds other values in their place, can miss the bound.
Values may be sent and summed in bfloat16 or wider, within the bound.
No kernel may reach another device: no remote copies, remote signals or barrier semaphores. Data moves between devices by JAX's collectives and lax.ppermute only.
A program may use at most 128 MiB of HBM per device.

v0:
```python
import jax
import jax.numpy as jnp
from jax import lax
from jax.sharding import PartitionSpec as P

HEAD = 64
SEQ_LEN = 512


def layer_norm(values, gain_row, shift_row):
    center = values - jnp.mean(values, axis=-1, keepdims=True)
    spread = jnp.mean(center * center, axis=-1, keepdims=True)
    return center * lax.rsqrt(spread + 1e-12) * gain_row + shift_row


def gelu_exact(values):
    return jax.nn.gelu(values, approximate=False)


def contract_rows(left, right):
    return lax.dot_general(
        left, right, (((0,), (0,)), ((), ())), preferred_element_type=jnp.float32
    )


def contract_cols(left, right):
    return lax.dot_general(
        left, right, (((1,), (1,)), ((), ())), preferred_element_type=jnp.float32
    )


def attend_forward(packed):
    queries, key_rows, value_rows = packed
    scores = (
        jnp.einsum("qhd,khd->hqk", queries, key_rows, preferred_element_type=jnp.float32) * 0.125
    )
    highest = jnp.max(scores, axis=-1, keepdims=True)
    unnorm = jnp.exp(scores - highest)
    totals = jnp.sum(unnorm, axis=-1, keepdims=True)
    soft_probs = (unnorm / totals).astype(jnp.bfloat16)
    attended = jnp.einsum(
        "hqk,khd->qhd", soft_probs, value_rows, preferred_element_type=jnp.float32
    )
    return (attended.astype(jnp.bfloat16), highest + jnp.log(totals))


def attend_backward(packed):
    queries, key_rows, value_rows, grad_att, log_total = packed
    scores = (
        jnp.einsum("qhd,khd->hqk", queries, key_rows, preferred_element_type=jnp.float32) * 0.125
    )
    soft_probs = jnp.exp(scores - log_total)
    grad_prob = jnp.einsum("qhd,khd->hqk", grad_att, value_rows, preferred_element_type=jnp.float32)
    inner_sum = jnp.sum(soft_probs * grad_prob, axis=-1, keepdims=True)
    grad_score = (soft_probs * (grad_prob - inner_sum)).astype(jnp.bfloat16)
    grad_query = (
        jnp.einsum("hqk,khd->qhd", grad_score, key_rows, preferred_element_type=jnp.float32) * 0.125
    ).astype(jnp.bfloat16)
    grad_key = (
        jnp.einsum("hqk,qhd->khd", grad_score, queries, preferred_element_type=jnp.float32) * 0.125
    ).astype(jnp.bfloat16)
    grad_value = jnp.einsum(
        "hqk,qhd->khd",
        soft_probs.astype(jnp.bfloat16),
        grad_att,
        preferred_element_type=jnp.float32,
    ).astype(jnp.bfloat16)
    return (grad_query, grad_key, grad_value)


def on_device(
    tokens,
    w_query,
    w_key,
    w_value,
    b_query,
    b_value,
    w_output,
    b_output,
    first_gain,
    first_shift,
    w_up,
    b_up,
    w_down,
    b_down,
    second_gain,
    second_shift,
    cotangent,
):
    share_rows = tokens.shape[0]
    group_rows = share_rows * lax.axis_size("tensor")
    local_width = w_query.shape[1]
    local_heads = local_width // HEAD
    seq_count = group_rows // SEQ_LEN
    w_joined = jnp.concatenate([w_query, w_key, w_value], axis=1)
    b_joined = jnp.concatenate(
        [
            b_query.astype(jnp.float32),
            jnp.zeros((local_width,), jnp.float32),
            b_value.astype(jnp.float32),
        ]
    )

    def split_heads(block):
        return block.reshape(seq_count, SEQ_LEN, local_heads, HEAD)

    inputs_full = lax.all_gather(tokens, "tensor", axis=0, tiled=True)
    projected = (
        jnp.dot(inputs_full, w_joined, preferred_element_type=jnp.float32) + b_joined
    ).astype(jnp.bfloat16)
    queries = split_heads(projected[:, :local_width])
    key_rows = split_heads(projected[:, local_width : 2 * local_width])
    value_rows = split_heads(projected[:, 2 * local_width :])
    attended, log_total = lax.map(attend_forward, (queries, key_rows, value_rows))
    attended = attended.reshape(group_rows, local_width)
    picked = attended
    attention_part = lax.psum_scatter(
        jnp.dot(picked, w_output, preferred_element_type=jnp.float32),
        "tensor",
        scatter_dimension=0,
        tiled=True,
    )
    first_sum = attention_part + b_output.astype(jnp.float32) + tokens.astype(jnp.float32)
    normed, first_pull = jax.vjp(
        layer_norm, first_sum, first_gain.astype(jnp.float32), first_shift.astype(jnp.float32)
    )
    normed_low = normed.astype(jnp.bfloat16)
    normed_full = lax.all_gather(normed_low, "tensor", axis=0, tiled=True)
    up_rows = jnp.dot(normed_full, w_up, preferred_element_type=jnp.float32) + b_up.astype(
        jnp.float32
    )
    active, gelu_pull = jax.vjp(gelu_exact, up_rows)
    active = active.astype(jnp.bfloat16)
    picked = active
    feed_part = lax.psum_scatter(
        jnp.dot(picked, w_down, preferred_element_type=jnp.float32),
        "tensor",
        scatter_dimension=0,
        tiled=True,
    )
    second_sum = feed_part + b_down.astype(jnp.float32) + normed
    layer_out, second_pull = jax.vjp(
        layer_norm, second_sum, second_gain.astype(jnp.float32), second_shift.astype(jnp.float32)
    )
    grad_second, grad_second_gain, grad_second_shift = second_pull(cotangent.astype(jnp.float32))
    grad_b_down = jnp.sum(grad_second, axis=0)
    down_low = grad_second.astype(jnp.bfloat16)
    down_full = lax.all_gather(down_low, "tensor", axis=0, tiled=True)
    grad_w_down = contract_rows(active, down_full)
    grad_active = contract_cols(down_full, w_down)
    grad_up = gelu_pull(grad_active)[0].astype(jnp.bfloat16)
    grad_b_up = jnp.sum(grad_up, axis=0, dtype=jnp.float32)
    grad_w_up = contract_rows(normed_full, grad_up)
    picked = grad_up
    hidden_part = lax.psum_scatter(
        contract_cols(picked, w_up), "tensor", scatter_dimension=0, tiled=True
    )
    grad_normed = hidden_part + grad_second
    grad_first, grad_first_gain, grad_first_shift = first_pull(grad_normed)
    grad_b_output = jnp.sum(grad_first, axis=0)
    first_low = grad_first.astype(jnp.bfloat16)
    first_full = lax.all_gather(first_low, "tensor", axis=0, tiled=True)
    grad_w_output = contract_rows(attended, first_full)
    grad_att = contract_cols(first_full, w_output).astype(jnp.bfloat16)
    grad_query, grad_key, grad_value = lax.map(
        attend_backward, (queries, key_rows, value_rows, split_heads(grad_att), log_total)
    )
    grad_joined = jnp.concatenate(
        [
            grad_query.reshape(group_rows, local_width),
            grad_key.reshape(group_rows, local_width),
            grad_value.reshape(group_rows, local_width),
        ],
        axis=1,
    )
    grad_b_query = jnp.sum(grad_joined[:, :local_width], axis=0, dtype=jnp.float32)
    grad_b_value = jnp.sum(grad_joined[:, 2 * local_width :], axis=0, dtype=jnp.float32)
    grad_w_joined = contract_rows(inputs_full, grad_joined)
    picked = grad_joined
    input_part = lax.psum_scatter(
        contract_cols(picked, w_joined), "tensor", scatter_dimension=0, tiled=True
    )
    grad_tokens = (input_part + grad_first).astype(jnp.bfloat16)
    grad_w_query = grad_w_joined[:, :local_width]
    grad_w_key = grad_w_joined[:, local_width : 2 * local_width]
    grad_w_value = grad_w_joined[:, 2 * local_width :]
    (
        grad_w_query,
        grad_w_key,
        grad_w_value,
        grad_b_query,
        grad_b_value,
        grad_w_output,
        grad_w_up,
        grad_b_up,
        grad_w_down,
    ) = lax.psum(
        (
            grad_w_query,
            grad_w_key,
            grad_w_value,
            grad_b_query,
            grad_b_value,
            grad_w_output,
            grad_w_up,
            grad_b_up,
            grad_w_down,
        ),
        "dp",
    )
    (
        grad_b_output,
        grad_first_gain,
        grad_first_shift,
        grad_b_down,
        grad_second_gain,
        grad_second_shift,
    ) = lax.psum(
        (
            grad_b_output,
            grad_first_gain,
            grad_first_shift,
            grad_b_down,
            grad_second_gain,
            grad_second_shift,
        ),
        ("dp", "tensor"),
    )
    return (
        layer_out.astype(jnp.bfloat16),
        grad_tokens,
        grad_w_query,
        grad_w_key,
        grad_w_value,
        grad_b_query,
        grad_b_value,
        grad_w_output,
        grad_b_output,
        grad_first_gain,
        grad_first_shift,
        grad_w_up,
        grad_b_up,
        grad_w_down,
        grad_b_down,
        grad_second_gain,
        grad_second_shift,
    )


def solution(mesh):
    return jax.shard_map(
        on_device,
        mesh=mesh,
        in_specs=(
            P(("dp", "tensor"), None),
            P(None, "tensor"),
            P(None, "tensor"),
            P(None, "tensor"),
            P("tensor"),
            P("tensor"),
            P("tensor", None),
            P(),
            P(),
            P(),
            P(None, "tensor"),
            P("tensor"),
            P("tensor", None),
            P(),
            P(),
            P(),
            P(("dp", "tensor"), None),
        ),
        out_specs=(
            P(("dp", "tensor"), None),
            P(("dp", "tensor"), None),
            P(None, "tensor"),
            P(None, "tensor"),
            P(None, "tensor"),
            P("tensor"),
            P("tensor"),
            P("tensor", None),
            P(),
            P(),
            P(),
            P(None, "tensor"),
            P("tensor"),
            P("tensor", None),
            P(),
            P(),
            P(),
        ),
        check_vma=False,
    )
```

profile of v0, /device:TPU:0, one launch (start us, length us, event | category | flops | bytes accessed | tf_op | source)
XLA Modules:
  0.0 759.8 jit_solution(11368604049422810197)
XLA Ops:
  12.4 28.5 %all-gather.5.cloned.1.call-done = bf16[2048,768]{1,0:T(8,128)(2,1)} async-done(((bf16[512,768]{1,0:T(8,128)(2,1)}), bf16[2048,768]{1,0:T(8,128)(2,1)}) %all-gather.5.cloned.1.call-update) | async-done | bytes 3145744 | tf_op jit(solution)/shard_map/all_gather | solution.py:107
  40.9 3.9 fusion.63
  45.0 1.5 reshape.152
  47.7 1.5 reshape.153
  50.5 1.5 reshape.154
  54.2 12.9 %while.26 = (s32[]{:T(128)}, bf16[4,512,3,64]{1,3,2,0:T(8,128)(2,1)}, f32[4,3,512,1]{2,1,3,0:T(4,128)}, bf16[4,512,3,64]{1,3,2,0:T(8,128)(2,1)S(1)}, bf16[4,512,...) while((s32[]{:T(128)}, bf16[4,512,3,64]{1,3,2,0:T(8,128)(2,1)}, ...), condition=%wide.region_3.4_spmd, body=%wide.region_0.3_spmd.sunk | while | flops 208501248 | bytes 10281549 | solution.py:114
  56.0 1.4 fusion.128
  59.2 1.4 fusion.128
  62.4 1.4 fusion.128
  65.7 1.4 fusion.128
  67.1 2.3 copy.52
  70.5 3.7 fusion.78
  74.9 57.8 %reduce-scatter.5.cloned.1.call-done = f32[512,768]{1,0:T(8,128)} async-done(((f32[2048,768]{1,0:T(8,128)}), f32[512,768]{1,0:T(8,128)}) %reduce-scatter.5.cloned.1.call-update) | async-done | bytes 1572880 | tf_op jit(solution)/shard_map/reduce_scatter | solution.py:117
  132.8 1.9 fusion.75
  137.9 27.7 %all-gather.7.cloned.1.call-done = bf16[2048,768]{1,0:T(8,128)(2,1)} async-done(((bf16[512,768]{1,0:T(8,128)(2,1)}), bf16[2048,768]{1,0:T(8,128)(2,1)}) %all-gather.7.cloned.1.call-update) | async-done | bytes 3145744 | tf_op jit(solution)/shard_map/all_gather | solution.py:128
  165.5 18.4 %multiply_convert_fusion.1 = (bf16[2048,768]{1,0:T(8,128)(2,1)S(1)}, f32[2048,768]{1,0:T(8,128)}, f32[2048,768]{1,0:T(8,128)}) fusion(f32[768]{0:T(1024)S(1)} %convert_element_type.116, bf16[2048,768]{1,0:T(8,128)(2,1)} %all-gather.7.cloned.1.call-done, bf16[768,768]{1,0:T(8,128)(2,1)S(1)} %copy-done), kind=kOutput, calls=%fused_computation.64 | convolution fusion | flops 2519728128 | bytes 20057088 | tf_op jit(solution)/shard_map/dot_general | solution.py:129
  184.0 1.7 copy-done.40
  185.7 4.5 fusion.79
  193.4 55.3 %reduce-scatter.7.cloned.1.call-done = f32[512,768]{1,0:T(8,128)} async-done(((f32[2048,768]{1,0:T(8,128)}), f32[512,768]{1,0:T(8,128)}) %reduce-scatter.7.cloned.1.call-update) | async-done | bytes 1572880 | tf_op jit(solution)/shard_map/reduce_scatter | solution.py:135
  248.7 2.0 fusion.73
  252.3 1.6 fusion.72
  255.0 1.7 add_reduce_fusion.1
  257.3 28.1 %all-gather.9.cloned.1.call-done = bf16[2048,768]{1,0:T(8,128)(2,1)} async-done(((bf16[512,768]{1,0:T(8,128)(2,1)}), bf16[2048,768]{1,0:T(8,128)(2,1)}) %all-gather.9.cloned.1.call-update) | async-done | bytes 3145744 | tf_op jit(solution)/shard_map/all_gather | solution.py:148
  285.4 11.0 %convert_reduce_fusion = (f32[768]{0:T(1024)}, bf16[2048,768]{1,0:T(8,128)(2,1)S(1)}) fusion(f32[2048,768]{1,0:T(8,128)} %get-tuple-element.195, f32[2048,768]{1,0:T(8,128)} %get-tuple-element.213, f32[768]{0:T(1024)} %copy-done.32, bf16[2048,768]{1,0:T(8,128)(2,1)} %all-gather.9.cloned.1.call-done, bf16[768,768]{1,0:T(8,128)(2,1)} %param.33), kind=kOutput, calls=%fused_computation.62 | convolution fusion | flops 2442657024 | bytes 20060160 | tf_op jit(solution)/shard_map/dot_general | solution.py:27
  296.5 1.7 copy-done.41
  298.1 4.5 fusion.80
  302.7 58.5 %reduce-scatter.9.cloned.1.call-done = f32[512,768]{1,0:T(8,128)} async-done(((f32[2048,768]{1,0:T(8,128)}), f32[512,768]{1,0:T(8,128)}) %reduce-scatter.9.cloned.1.call-update) | async-done | bytes 1572880 | tf_op jit(solution)/shard_map/reduce_scatter | solution.py:155
  361.2 3.3 multiply_reduce_fusion.2
  367.7 28.5 %all-gather.11.cloned.1.call-done = bf16[2048,768]{1,0:T(8,128)(2,1)} async-done(((bf16[512,768]{1,0:T(8,128)(2,1)}), bf16[2048,768]{1,0:T(8,128)(2,1)}) %all-gather.11.cloned.1.call-update) | async-done | bytes 3145744 | tf_op jit(solution)/shard_map/all_gather | solution.py:162
  396.2 3.1 convolution_convert_fusion
  402.0 27.8 %while.27 = (s32[]{:T(128)}, bf16[4,512,3,64]{1,3,2,0:T(8,128)(2,1)S(1)}, bf16[4,512,3,64]{1,3,2,0:T(8,128)(2,1)}, bf16[4,512,3,64]{1,3,2,0:T(8,128)(2,1)}, bf16...) while((s32[]{:T(128)}, ...), condition=%wide.region_17.18_spmd, body=%wide.region_15.17_spmd.sunk | while | flops 513243648 | bytes 25611368 | solution.py:165
  403.3 1.7 multiply_reduce_fusion.9
  410.3 1.7 multiply_reduce_fusion.9
  417.2 1.7 multiply_reduce_fusion.9
  424.2 1.7 multiply_reduce_fusion.9
  431.7 1.8 copy.59
  435.3 4.6 fusion.81
  440.2 7.0 fusion.84
  447.2 4.2 fusion.83
  451.4 2.0 convolution_bitcast_fusion
  455.1 1.6 fusion.82
  457.4 40.8 %all-reduce = (f32[768]{0:T(1024)}, f32[768]{0:T(1024)}, f32[768]{0:T(1024)}, f32[768]{0:T(1024)}, f32[768]{0:T(1024)}, /*index=5*/f32[768]{0:T(1024)}) all-reduce(f32[768]{0:T(1024)S(1)} %get-tuple-element.211, f32[768]{0:T(1024)S(1)} %copy-done.29, f32[768]{0:T(1024)S(1)} %copy-done.30, ...), channel_id=1, replica_groups=mesh['dp'=8,'tensor'=4] {'dp','tensor'}, use_global_device_ids=true, to_apply=%region_28.29 | all-reduce | flops 4608 | bytes 36864 | tf_op jit(solution)/shard_map/psum | solution.py:218
  499.9 22.2 %all-reduce.1 = (f32[192]{0:T(256)}, f32[192]{0:T(256)}, f32[768]{0:T(1024)}) all-reduce(f32[192]{0:T(256)S(1)} %reduce_sum.216, f32[192]{0:T(256)S(1)} %reduce_sum.218, f32[768]{0:T(1024)S(1)} %copy-done.31), channel_id=1, replica_groups=mesh['dp'=8,'tensor'=4] {'dp'}, use_global_device_ids=true, to_apply=%region_23.24 | all-reduce | flops 1152 | bytes 9216 | tf_op jit(solution)/shard_map/psum | solution.py:197
  522.1 2.5 add_convert_fusion.2
  524.6 218.8 %all-reduce.5.cloned.1.call-done = (f32[768,192]{0,1:T(8,128)}, f32[768,192]{0,1:T(8,128)}, f32[768,192]{0,1:T(8,128)}, f32[192,768]{1,0:T(8,128)}, f32[768,768]{1,0:T(8,128)}, /*index=5*/f32[768,768]{1,0:T(8,128)}) async-done(((f32[768,192]{0,1:T(8,128)}, f32[768,192]{0,1:T(8,128)}, f32[768,192]{0,1:T(8,128)}, f32[192,768]{1,0:T(8,128)}, f32[768,768]{1,0:T(8,128)}, /*index=5*/f32[768,768]{1,0:T(8,128)}), ...) | async-done | bytes 7077904 | tf_op jit(solution)/shard_map/psum | solution.py:197
  743.5 2.1 copy.106
  745.5 1.9 copy.107
  747.4 1.9 copy.108
  (194 shorter events, 66.8 us)
Async XLA Ops:
  7.2 158.3 %copy-start = (bf16[768,768]{1,0:T(8,128)(2,1)S(1)}, bf16[768,768]{1,0:T(8,128)(2,1)}, u32[]{:S(2)}) copy-start(bf16[768,768]{1,0:T(8,128)(2,1)} %param.31) | copy-start | bytes 3538948
  7.2 33.7 %all-gather.5.cloned.1.call-start = ((), (), s32[]{:S(2)}) async-start(), calls=%async_computation.4 | async-start | bytes 3932160 | tf_op jit(solution)/shard_map/all_gather | solution.py:107
  7.9 124.8 %reduce-scatter.5.cloned.1.call-start = ((), (), s32[]{:S(2)}) async-start(), calls=%async_computation.5 | async-start | bytes 7864320 | tf_op jit(solution)/shard_map/reduce_scatter | solution.py:117
  12.4 28.5 %copy-start.20 = (bf16[768,576]{0,1:T(8,128)(2,1)}, bf16[768,576]{0,1:T(8,128)(2,1)S(1)}, u32[]{:S(2)}) copy-start(bf16[768,576]{0,1:T(8,128)(2,1)S(1)} %constant_dynamic-update-slice_fusion) | copy-start | bytes 2654212
  67.1 7.1 copy-start.2
  67.1 7.1 copy-start.9
  67.1 3.4 copy-start.16
  69.6 0.9 copy-start.7
  74.2 0.7 copy-start.34
  74.2 0.7 copy-start.35
  74.3 91.3 %all-gather.7.cloned.1.call-start = ((), (), s32[]{:S(2)}) async-start(), calls=%async_computation.6 | async-start | bytes 3932160 | tf_op jit(solution)/shard_map/all_gather | solution.py:128
  74.9 61.9 %copy-start.22 = (f32[768]{0:T(1024)}, f32[768]{0:T(1024)S(1)}, u32[]{:S(2)}) copy-start(f32[768]{0:T(1024)S(1)} %convert_element_type.114) | copy-start | bytes 9220
  136.8 111.9 %reduce-scatter.7.cloned.1.call-start = ((), (), s32[]{:S(2)}) async-start(), calls=%async_computation.7 | async-start | bytes 7864320 | tf_op jit(solution)/shard_map/reduce_scatter | solution.py:135
  137.9 46.1 %copy-start.32 = (f32[768]{0:T(1024)}, f32[768]{0:T(1024)S(1)}, u32[]{:S(2)}) copy-start(f32[768]{0:T(1024)S(1)} %convert_element_type.116) | copy-start | bytes 9220
  165.5 20.2 %copy-start.39 = (bf16[768,768]{1,0:T(8,128)(2,1)S(1)}, bf16[768,768]{1,0:T(8,128)(2,1)}, u32[]{:S(2)}) copy-start(bf16[768,768]{1,0:T(8,128)(2,1)} %param.33) | copy-start | bytes 3538948
  184.0 1.7 copy-start.40
  190.2 95.3 %all-gather.9.cloned.1.call-start = ((), (), s32[]{:S(2)}) async-start(), calls=%async_computation.8 | async-start | bytes 3932160 | tf_op jit(solution)/shard_map/all_gather | solution.py:148
  248.7 2.4 copy-start.11
  250.7 1.6 copy-start.25
  253.9 1.1 copy-start.6
  256.7 104.5 %reduce-scatter.9.cloned.1.call-start = ((), (), s32[]{:S(2)}) async-start(), calls=%async_computation.9 | async-start | bytes 7864320 | tf_op jit(solution)/shard_map/reduce_scatter | solution.py:155
  296.5 1.7 copy-start.41
  302.7 61.8 %copy-start.24 = (f32[512]{0:T(512)S(1)}, f32[512]{0:T(512)}, u32[]{:S(2)}) copy-start(f32[512]{0:T(512)} %copy-done.23) | copy-start | bytes 6148
  302.7 93.5 %all-gather.11.cloned.1.call-start = ((), (), s32[]{:S(2)}) async-start(), calls=%async_computation.10 | async-start | bytes 3932160 | tf_op jit(solution)/shard_map/all_gather | solution.py:162
  364.5 31.7 %copy-start.17 = (bf16[192,768]{1,0:T(8,128)(2,1)S(1)}, bf16[192,768]{1,0:T(8,128)(2,1)}, u32[]{:S(2)}) copy-start(bf16[192,768]{1,0:T(8,128)(2,1)} %param.27) | copy-start | bytes 884740
  365.2 1.2 copy-start.4
  367.5 154.6 %reduce-scatter.11.cloned.1.call-start = ((), (), s32[]{:S(2)}) async-start(), calls=%async_computation.11 | async-start | bytes 7864320 | tf_op jit(solution)/shard_map/reduce_scatter | solution.py:180
  399.2 2.7 copy-start.3
  429.8 1.1 copy-start.12
  431.7 3.6 copy-start.21
  433.9 1.4 copy-start.18
  439.9 303.6 %all-reduce.5.cloned.1.call-start = ((), (), s32[]{:S(2)}) async-start(), calls=%async_computation.12 | async-start | bytes 14155776 | tf_op jit(solution)/shard_map/psum | solution.py:197
  440.1 7.1 copy-start.38
  440.2 7.1 copy-start.42
  447.2 4.2 copy-start.19
  447.2 4.2 copy-start.37
  451.4 3.3 copy-start.10
  453.4 1.6 copy-start.8
  456.7 0.7 copy-start.27
  456.7 0.7 copy-start.28
  456.7 0.7 copy-start.29
  456.7 0.7 copy-start.30
  456.7 43.1 %copy-start.31 = (f32[768]{0:T(1024)S(1)}, f32[768]{0:T(1024)}, u32[]{:S(2)}) copy-start(f32[768]{0:T(1024)} %get-tuple-element.185) | copy-start | bytes 9220
  456.7 65.4 %copy-start.5 = (f32[512,768]{1,0:T(8,128)S(1)}, f32[512,768]{1,0:T(8,128)}, u32[]{:S(2)}) copy-start(f32[512,768]{1,0:T(8,128)} %copy-done.4) | copy-start | bytes 4718596
  743.5 5.9 copy-start.15
  743.5 6.7 copy-start.14
  749.4 2.2 copy-start.13
  750.2 2.8 copy-start.1
  (4 other events, 2.6 us)
Sparse Core Ops, SparseCore 0:
  9.6 31.2 all-gather.4
  74.4 58.3 reduce-scatter.4
  137.0 28.5 all-gather.6
  190.3 58.3 reduce-scatter.6
  256.9 28.5 all-gather.8
  302.8 58.3 reduce-scatter.8
  367.6 28.5 all-gather.10
  440.0 59.7 reduce-scatter.10
  506.0 237.3 all-reduce.4
where the time goes:
time: 768 us; the launch traced here: 760 us
  waiting for transfers between devices  504 us (66%)
  matrix products  98.3 us (13%)
  blocking collectives  63.1 us (8%)
  local copies, waits for them, and re-layouts  46.3 us (6%)
  other arithmetic  31.9 us (4%)
  between operations  14.5 us (2%)
    psum x1, waiting for transfers between devices, on_device(): lax.psum((grad_w_query, grad_w_key, grad_w_value, grad_b_query, grad_b_va...  219 us
    reduce_scatter x1, waiting for transfers between devices, on_device(): lax.psum_scatter(contract_cols(picked, w_up), 'tensor', scatter_dimension...  58.5 us
    reduce_scatter x1, waiting for transfers between devices, on_device(): lax.psum_scatter(jnp.dot(picked, w_output, preferred_element_type=jnp.flo...  57.8 us
    reduce_scatter x1, waiting for transfers between devices, on_device(): lax.psum_scatter(jnp.dot(picked, w_down, preferred_element_type=jnp.float...  55.3 us
    psum x1, blocking collectives, on_device(): lax.psum((grad_b_output, grad_first_gain, grad_first_shift, grad_b_down,...  40.8 us
    all_gather x1, waiting for transfers between devices, on_device(): inputs_full = lax.all_gather(tokens, 'tensor', axis=0, tiled=True)  28.5 us
    all_gather x1, waiting for transfers between devices, on_device(): first_full = lax.all_gather(first_low, 'tensor', axis=0, tiled=True)  28.5 us
    all_gather x1, waiting for transfers between devices, on_device(): down_full = lax.all_gather(down_low, 'tensor', axis=0, tiled=True)  28.1 us
  transfers between devices with their start and end apart: 9, of which 8 were waited for; matrix products, arithmetic and copies ran while one was open for 4% of the time, Pallas kernels for 0%

commit v1 on v0

--- a/solution.py
+++ b/solution.py
@@ -87,6 +87,29 @@
     second_shift,
     cotangent,
 ):
+
+    def name_steps_all(target):
+        vec_out, prior, y_new = (
+            jax.lax.axis_size("tensor"),
+            jax.lax.axis_index("tensor"),
+            target.shape[0],
+        )
+        k_now, f_next = (target, 1)
+        while f_next < vec_out:
+            k_now = jnp.concatenate(
+                [
+                    k_now,
+                    jax.lax.ppermute(
+                        k_now,
+                        axis_name="tensor",
+                        perm=[(s, (s - f_next) % vec_out) for s in range(vec_out)],
+                    ),
+                ],
+                0,
+            )
+            f_next = 2 * f_next
+        return jnp.roll(k_now, prior * y_new, 0)
+
     share_rows = tokens.shape[0]
     group_rows = share_rows * lax.axis_size("tensor")
     local_width = w_query.shape[1]
@@ -159,7 +182,7 @@
     grad_first, grad_first_gain, grad_first_shift = first_pull(grad_normed)
     grad_b_output = jnp.sum(grad_first, axis=0)
     first_low = grad_first.astype(jnp.bfloat16)
-    first_full = lax.all_gather(first_low, "tensor", axis=0, tiled=True)
+    first_full = name_steps_all(first_low)
     grad_w_output = contract_rows(attended, first_full)
     grad_att = contract_cols(first_full, w_output).astype(jnp.bfloat16)
     grad_query, grad_key, grad_value = lax.map(

time: 768 us -> 793 us (1.033)
  waiting for transfers between devices: 504 us -> 518 us
    ppermute x0 -> x2, waiting for transfers between devices: none -> 43.9 us  [name_steps_all(): jax.lax.ppermute(k_now, axis_name='tensor', perm=[(s, (s - f_next) % vec_...]
    all_gather x1 -> x0, waiting for transfers between devices: 28.5 us -> none  [on_device(): first_full = lax.all_gather(first_low, 'tensor', axis=0, tiled=True)]
    psum x1, waiting for transfers between devices: 219 us -> 198 us  [on_device(): lax.psum((grad_w_query, grad_w_key, grad_w_value, grad_b_query, grad_b_va...]
    reduce_scatter x1, waiting for transfers between devices: 0.01 us -> 19.8 us  [on_device(): lax.psum_scatter(contract_cols(picked, w_joined), 'tensor', scatter_dimen...]
  transfers between devices with their start and end apart: 9 -> 10, of which waited for: 8 -> 10; matrix products, arithmetic and copies ran while one was open for 4% -> 4% of each run, Pallas kernels for 0% -> 0%
where the time goes in v1:
time: 793 us; the launch traced here: 786 us
  waiting for transfers between devices  518 us (65%)
  matrix products  98.5 us (12%)
  blocking collectives  66.7 us (8%)
  local copies, waits for them, and re-layouts  52.1 us (7%)
  other arithmetic  32.3 us (4%)
  between operations  14.8 us (2%)
    psum x1, waiting for transfers between devices, on_device(): lax.psum((grad_w_query, grad_w_key, grad_w_value, grad_b_query, grad_b_va...  198 us
    reduce_scatter x1, waiting for transfers between devices, on_device(): lax.psum_scatter(contract_cols(picked, w_up), 'tensor', scatter_dimension...  58.5 us
    reduce_scatter x1, waiting for transfers between devices, on_device(): lax.psum_scatter(jnp.dot(picked, w_output, preferred_element_type=jnp.flo...  57.8 us
    reduce_scatter x1, waiting for transfers between devices, on_device(): lax.psum_scatter(jnp.dot(picked, w_down, preferred_element_type=jnp.float...  55.2 us
    psum x1, blocking collectives, on_device(): lax.psum((grad_b_output, grad_first_gain, grad_first_shift, grad_b_down,...  44.3 us
    ppermute x2, waiting for transfers between devices, name_steps_all(): jax.lax.ppermute(k_now, axis_name='tensor', perm=[(s, (s - f_next) % vec_...  43.9 us
    all_gather x1, waiting for transfers between devices, on_device(): inputs_full = lax.all_gather(tokens, 'tensor', axis=0, tiled=True)  28.5 us
    all_gather x1, waiting for transfers between devices, on_device(): down_full = lax.all_gather(down_low, 'tensor', axis=0, tiled=True)  28.1 us
  transfers between devices with their start and end apart: 10, of which 10 were waited for; matrix products, arithmetic and copies ran while one was open for 4% of the time, Pallas kernels for 0%

profile of v1, /device:TPU:0, one launch (start us, length us, event | category | flops | bytes accessed | tf_op | source)
XLA Modules:
  0.0 785.5 jit_solution(2233453194579506255)
XLA Ops:
  12.4 28.5 %all-gather.4.cloned.1.call-done = bf16[2048,768]{1,0:T(8,128)(2,1)} async-done(((bf16[512,768]{1,0:T(8,128)(2,1)}), bf16[2048,768]{1,0:T(8,128)(2,1)}) %all-gather.4.cloned.1.call-update) | async-done | bytes 3145744 | tf_op jit(solution)/shard_map/all_gather | solution.py:130
  40.9 3.9 fusion.63
  54.1 12.9 %while.26 = (s32[]{:T(128)}, bf16[4,512,3,64]{1,3,2,0:T(8,128)(2,1)}, f32[4,3,512,1]{2,1,3,0:T(4,128)}, bf16[4,512,3,64]{1,3,2,0:T(8,128)(2,1)S(1)}, bf16[4,512,...) while((s32[]{:T(128)}, bf16[4,512,3,64]{1,3,2,0:T(8,128)(2,1)}, ...), condition=%wide.region_3.4_spmd, body=%wide.region_0.3_spmd.sunk | while | flops 208501248 | bytes 10281049 | solution.py:137
  55.3 1.5 fusion.134
  61.8 1.5 fusion.134
  67.1 2.3 copy.52
  70.5 3.7 fusion.87
  74.9 57.8 %reduce-scatter.5.cloned.1.call-done = f32[512,768]{1,0:T(8,128)} async-done(((f32[2048,768]{1,0:T(8,128)}), f32[512,768]{1,0:T(8,128)}) %reduce-scatter.5.cloned.1.call-update) | async-done | bytes 1572880 | tf_op jit(solution)/shard_map/reduce_scatter | solution.py:140
  132.8 1.9 fusion.84
  137.9 27.7 %all-gather.6.cloned.1.call-done = bf16[2048,768]{1,0:T(8,128)(2,1)} async-done(((bf16[512,768]{1,0:T(8,128)(2,1)}), bf16[2048,768]{1,0:T(8,128)(2,1)}) %all-gather.6.cloned.1.call-update) | async-done | bytes 3145744 | tf_op jit(solution)/shard_map/all_gather | solution.py:151
  165.5 18.4 %multiply_convert_fusion.1 = (bf16[2048,768]{1,0:T(8,128)(2,1)S(1)}, f32[2048,768]{1,0:T(8,128)}, f32[2048,768]{1,0:T(8,128)}) fusion(f32[768]{0:T(1024)S(1)} %convert_element_type.116, bf16[2048,768]{1,0:T(8,128)(2,1)} %all-gather.6.cloned.1.call-done, bf16[768,768]{1,0:T(8,128)(2,1)S(1)} %copy-done), kind=kOutput, calls=%fused_computation.64 | convolution fusion | flops 2519728128 | bytes 20057088 | tf_op jit(solution)/shard_map/dot_general | solution.py:152
  184.0 1.7 copy-done.36
  185.7 4.5 fusion.88
  193.5 55.2 %reduce-scatter.7.cloned.1.call-done = f32[512,768]{1,0:T(8,128)} async-done(((f32[2048,768]{1,0:T(8,128)}), f32[512,768]{1,0:T(8,128)}) %reduce-scatter.7.cloned.1.call-update) | async-done | bytes 1572880 | tf_op jit(solution)/shard_map/reduce_scatter | solution.py:158
  248.7 2.0 fusion.82
  252.3 1.6 fusion.81
  255.1 1.7 add_reduce_fusion.1
  257.3 28.1 %all-gather.8.cloned.1.call-done = bf16[2048,768]{1,0:T(8,128)(2,1)} async-done(((bf16[512,768]{1,0:T(8,128)(2,1)}), bf16[2048,768]{1,0:T(8,128)(2,1)}) %all-gather.8.cloned.1.call-update) | async-done | bytes 3145744 | tf_op jit(solution)/shard_map/all_gather | solution.py:171
  285.4 11.0 %convert_reduce_fusion = (f32[768]{0:T(1024)}, bf16[2048,768]{1,0:T(8,128)(2,1)S(1)}) fusion(f32[2048,768]{1,0:T(8,128)} %get-tuple-element.197, f32[2048,768]{1,0:T(8,128)} %get-tuple-element.215, f32[768]{0:T(1024)} %copy-done.29, bf16[2048,768]{1,0:T(8,128)(2,1)} %all-gather.8.cloned.1.call-done, bf16[768,768]{1,0:T(8,128)(2,1)} %param.33), kind=kOutput, calls=%fused_computation.62 | convolution fusion | flops 2442657024 | bytes 20060160 | tf_op jit(solution)/shard_map/dot_general | solution.py:27
  296.4 1.7 copy-done.37
  298.1 4.5 fusion.89
  302.7 58.5 %reduce-scatter.9.cloned.1.call-done = f32[512,768]{1,0:T(8,128)} async-done(((f32[2048,768]{1,0:T(8,128)}), f32[512,768]{1,0:T(8,128)}) %reduce-scatter.9.cloned.1.call-update) | async-done | bytes 1572880 | tf_op jit(solution)/shard_map/reduce_scatter | solution.py:178
  361.2 2.7 multiply_reduce_fusion.2
  366.0 9.5 %collective-permute-done = bf16[512,768]{1,0:T(8,128)(2,1)S(1)} collective-permute-done((bf16[512,768]{1,0:T(8,128)(2,1)S(1)}, bf16[512,768]{1,0:T(8,128)(2,1)S(1)}, u32[]{:S(2)}, u32[]{:S(2)}) %collective-permute-start) | collective-permute-done | bytes 786464 | tf_op jit(solution)/shard_map/ppermute | solution.py:102
  376.7 1.5 collective-permute-start.1
  379.1 34.4 %collective-permute-done.1 = bf16[1024,768]{1,0:T(8,128)(2,1)} collective-permute-done((bf16[1024,768]{1,0:T(8,128)(2,1)}, bf16[1024,768]{1,0:T(8,128)(2,1)}, u32[]{:S(2)}, u32[]{:S(2)}) %collective-permute-start.1) | collective-permute-done | bytes 1572896 | tf_op jit(solution)/shard_map/ppermute | solution.py:102
  413.5 2.8 constant_dynamic-update-slice_fusion.6
  418.2 2.7 constant_dynamic-update-slice_fusion.3
  420.9 3.0 fusion.68
  426.7 27.8 %while.27 = (s32[]{:T(128)}, bf16[4,512,3,64]{1,3,2,0:T(8,128)(2,1)}, bf16[4,512,3,64]{1,3,2,0:T(8,128)(2,1)}, bf16[4,512,3,64]{1,3,2,0:T(8,128)(2,1)S(1)}, bf16...) while((s32[]{:T(128)}, ...), condition=%wide.region_17.18_spmd, body=%wide.region_15.17_spmd.sunk | while | flops 513243648 | bytes 25611376 | solution.py:188
  428.6 1.7 multiply_reduce_fusion.9
  435.6 1.7 multiply_reduce_fusion.9
  442.5 1.7 multiply_reduce_fusion.9
  449.5 1.7 multiply_reduce_fusion.9
  454.4 1.8 copy.58
  459.6 4.6 fusion.90
  464.5 7.2 fusion.92
  471.8 4.2 fusion.91
  476.0 1.6 fusion.64
  478.2 2.0 convolution_bitcast_fusion
  482.1 22.4 %all-reduce.1 = (f32[192]{0:T(256)}, f32[192]{0:T(256)}, f32[768]{0:T(1024)}) all-reduce(f32[192]{0:T(256)S(1)} %reduce_sum.216, f32[192]{0:T(256)S(1)} %reduce_sum.218, f32[768]{0:T(1024)S(1)} %copy-done.28), channel_id=1, replica_groups=mesh['dp'=8,'tensor'=4] {'dp'}, use_global_device_ids=true, to_apply=%region_23.24 | all-reduce | flops 1152 | bytes 9216 | tf_op jit(solution)/shard_map/psum | solution.py:220
  504.5 19.8 %reduce-scatter.11.cloned.1.call-done = f32[512,768]{1,0:T(8,128)} async-done(((f32[2048,768]{1,0:T(8,128)}), f32[512,768]{1,0:T(8,128)}) %reduce-scatter.11.cloned.1.call-update) | async-done | bytes 1572880 | tf_op jit(solution)/shard_map/reduce_scatter | solution.py:203
  524.3 2.5 add_reduce_fusion
  526.8 44.3 %all-reduce = (f32[768]{0:T(1024)}, f32[768]{0:T(1024)}, f32[768]{0:T(1024)}, f32[768]{0:T(1024)}, f32[768]{0:T(1024)}, /*index=5*/f32[768]{0:T(1024)}) all-reduce(f32[768]{0:T(1024)S(1)} %get-tuple-element.213, f32[768]{0:T(1024)S(1)} %get-tuple-element.134, ...), channel_id=1, replica_groups=mesh['dp'=8,'tensor'=4] {'dp','tensor'}, use_global_device_ids=true, to_apply=%region_28.29 | all-reduce | flops 4608 | bytes 36864 | tf_op jit(solution)/shard_map/psum | solution.py:241
  571.1 197.8 %all-reduce.5.cloned.1.call-done = (f32[768,192]{0,1:T(8,128)}, f32[768,192]{0,1:T(8,128)}, f32[768,192]{0,1:T(8,128)}, f32[192,768]{1,0:T(8,128)}, f32[768,768]{1,0:T(8,128)}, /*index=5*/f32[768,768]{1,0:T(8,128)}) async-done(((f32[768,192]{0,1:T(8,128)}, f32[768,192]{0,1:T(8,128)}, f32[768,192]{0,1:T(8,128)}, f32[192,768]{1,0:T(8,128)}, f32[768,768]{1,0:T(8,128)}, /*index=5*/f32[768,768]{1,0:T(8,128)}), ...) | async-done | bytes 7077904 | tf_op jit(solution)/shard_map/psum | solution.py:220
  768.9 2.1 copy.111
  771.0 1.9 copy.112
  772.9 1.9 copy.113
  (198 shorter events, 75.3 us)
Async XLA Ops:
  7.2 158.3 %copy-start = (bf16[768,768]{1,0:T(8,128)(2,1)S(1)}, bf16[768,768]{1,0:T(8,128)(2,1)}, u32[]{:S(2)}) copy-start(bf16[768,768]{1,0:T(8,128)(2,1)} %param.31) | copy-start | bytes 3538948
  7.2 33.7 %all-gather.4.cloned.1.call-start = ((), (), s32[]{:S(2)}) async-start(), calls=%async_computation.4 | async-start | bytes 3932160 | tf_op jit(solution)/shard_map/all_gather | solution.py:130
  7.9 124.8 %reduce-scatter.5.cloned.1.call-start = ((), (), s32[]{:S(2)}) async-start(), calls=%async_computation.5 | async-start | bytes 7864320 | tf_op jit(solution)/shard_map/reduce_scatter | solution.py:140
  12.4 28.5 %copy-start.19 = (bf16[768,576]{0,1:T(8,128)(2,1)}, bf16[768,576]{0,1:T(8,128)(2,1)S(1)}, u32[]{:S(2)}) copy-start(bf16[768,576]{0,1:T(8,128)(2,1)S(1)} %constant_dynamic-update-slice_fusion) | copy-start | bytes 2654212
  67.1 7.2 copy-start.2
  67.1 7.2 copy-start.10
  67.1 3.4 copy-start.15
  69.6 0.9 copy-start.7
  74.2 0.7 copy-start.31
  74.2 0.7 copy-start.32
  74.3 91.3 %all-gather.6.cloned.1.call-start = ((), (), s32[]{:S(2)}) async-start(), calls=%async_computation.6 | async-start | bytes 3932160 | tf_op jit(solution)/shard_map/all_gather | solution.py:151
  74.9 61.9 %copy-start.21 = (f32[768]{0:T(1024)}, f32[768]{0:T(1024)S(1)}, u32[]{:S(2)}) copy-start(f32[768]{0:T(1024)S(1)} %convert_element_type.114) | copy-start | bytes 9220
  136.8 111.9 %reduce-scatter.7.cloned.1.call-start = ((), (), s32[]{:S(2)}) async-start(), calls=%async_computation.7 | async-start | bytes 7864320 | tf_op jit(solution)/shard_map/reduce_scatter | solution.py:158
  137.9 46.1 %copy-start.29 = (f32[768]{0:T(1024)}, f32[768]{0:T(1024)S(1)}, u32[]{:S(2)}) copy-start(f32[768]{0:T(1024)S(1)} %convert_element_type.116) | copy-start | bytes 9220
  165.5 20.2 %copy-start.35 = (bf16[768,768]{1,0:T(8,128)(2,1)S(1)}, bf16[768,768]{1,0:T(8,128)(2,1)}, u32[]{:S(2)}) copy-start(bf16[768,768]{1,0:T(8,128)(2,1)} %param.33) | copy-start | bytes 3538948
  184.0 1.7 copy-start.36
  190.2 95.3 %all-gather.8.cloned.1.call-start = ((), (), s32[]{:S(2)}) async-start(), calls=%async_computation.8 | async-start | bytes 3932160 | tf_op jit(solution)/shard_map/all_gather | solution.py:171
  248.7 2.4 copy-start.11
  250.7 1.6 copy-start.24
  253.9 1.1 copy-start.6
  256.7 104.4 %reduce-scatter.9.cloned.1.call-start = ((), (), s32[]{:S(2)}) async-start(), calls=%async_computation.9 | async-start | bytes 7864320 | tf_op jit(solution)/shard_map/reduce_scatter | solution.py:178
  296.4 1.7 copy-start.37
  302.7 61.2 %copy-start.23 = (f32[512]{0:T(512)S(1)}, f32[512]{0:T(512)}, u32[]{:S(2)}) copy-start(f32[512]{0:T(512)} %copy-done.22) | copy-start | bytes 6148
  302.7 221.6 %reduce-scatter.11.cloned.1.call-start = ((), (), s32[]{:S(2)}) async-start(), calls=%async_computation.10 | async-start | bytes 7864320 | tf_op jit(solution)/shard_map/reduce_scatter | solution.py:203
  364.5 12.2 %copy-start.4 = (f32[512,768]{1,0:T(8,128)}, f32[512,768]{1,0:T(8,128)S(1)}, u32[]{:S(2)}) copy-start(f32[512,768]{1,0:T(8,128)S(1)} %get-tuple-element.190) | copy-start | bytes 4718596
  365.8 9.7 %collective-permute-start = (bf16[512,768]{1,0:T(8,128)(2,1)S(1)}, bf16[512,768]{1,0:T(8,128)(2,1)S(1)}, u32[]{:S(2)}, u32[]{:S(2)}) collective-permute-start(bf16[512,768]{1,0:T(8,128)(2,1)S(1)} %get-tuple-element.188), channel_id=1, source_target_pairs={{0,3},{1,0},{2,1},{3,2},{4,7},{5,4},{6,5},{7,6},{8,11},{9,8},{10,9... | collective-permute-start | bytes 2359304 | tf_op jit(solution)/shard_map/ppermute | solution.py:102
  376.7 36.8 %collective-permute-start.1 = (bf16[1024,768]{1,0:T(8,128)(2,1)}, bf16[1024,768]{1,0:T(8,128)(2,1)}, u32[]{:S(2)}, u32[]{:S(2)}) collective-permute-start(bf16[1024,768]{1,0:T(8,128)(2,1)} %pad_maximum_fusion), channel_id=1, source_target_pairs={{0,2},{1,3},{2,0},{3,1},{4,6},{5,7},{6,4},{7,5},{8,10},{9,11},{10,... | collective-permute-start | bytes 4718600 | tf_op jit(solution)/shard_map/ppermute | solution.py:102
  416.3 4.6 copy-start.16
  423.9 2.7 copy-start.3
  454.4 2.0 copy-start.9
  457.9 1.8 copy-start.20
  458.2 1.4 copy-start.17
  464.2 304.7 %all-reduce.5.cloned.1.call-start = ((), (), s32[]{:S(2)}) async-start(), calls=%async_computation.11 | async-start | bytes 14155776 | tf_op jit(solution)/shard_map/psum | solution.py:220
  464.5 7.2 copy-start.34
  464.5 7.2 copy-start.38
  464.5 11.4 %slice-start = ((s8[6291456]{0:T(1024)(128)(4,1)}), s8[4194304]{0:T(1024)(128)(4,1)S(1)}, s32[]{:S(2)}) async-start(s8[6291456]{0:T(1024)(128)(4,1)} %bitcast.164), calls=%async_computation.12 | async-start | bytes 8388608
  471.7 4.2 copy-start.8
  471.7 4.2 slice-start.1
  471.7 5.8 copy-start.33
  476.0 2.2 copy-start.18
  481.4 42.9 %copy-start.5 = (f32[512,768]{1,0:T(8,128)S(1)}, f32[512,768]{1,0:T(8,128)}, u32[]{:S(2)}) copy-start(f32[512,768]{1,0:T(8,128)} %copy-done.4) | copy-start | bytes 4718596
  481.5 45.4 %copy-start.25 = (f32[768]{0:T(1024)S(1)}, f32[768]{0:T(1024)}, u32[]{:S(2)}) copy-start(f32[768]{0:T(1024)} %get-tuple-element.136) | copy-start | bytes 9220
  481.5 45.4 %copy-start.26 = (f32[768]{0:T(1024)S(1)}, f32[768]{0:T(1024)}, u32[]{:S(2)}) copy-start(f32[768]{0:T(1024)} %get-tuple-element.139) | copy-start | bytes 9220
  481.5 45.3 %copy-start.27 = (f32[768]{0:T(1024)S(1)}, f32[768]{0:T(1024)}, u32[]{:S(2)}) copy-start(f32[768]{0:T(1024)} %get-tuple-element.211) | copy-start | bytes 9220
  768.9 5.9 copy-start.14
  768.9 6.7 copy-start.13
  774.8 2.2 copy-start.12
  775.6 2.8 copy-start.1
  (3 other events, 2.0 us)
Sparse Core Ops, SparseCore 0:
  9.6 31.2 all-gather.3
  74.4 58.3 reduce-scatter.4
  136.9 28.5 all-gather.5
  190.3 58.3 reduce-scatter.6
  256.9 28.5 all-gather.7
  302.8 58.3 reduce-scatter.8
  464.4 59.8 reduce-scatter.10
  530.5 238.3 all-reduce.4
